TPU v7x, 512 devices: a whole 4x8x8 slice. The times are simulated.
512 devices in a mesh: dp: 8 (over y), seq: 64 (over z, x, core).
Axes of the slice: x: 4, y: 8, z: 8, core: 2. Of those that a mesh axis runs over, the one named last changes fastest.
Arguments:
- mel_frames: bfloat16 [8, 16384, 128], P('dp', 'seq'), may hold values from -16 to 16
- positions: int32 [8, 8192], P('dp', 'seq'), may hold values from 0 to 16383, as said below
- conv_weight: bfloat16 [128, 3, 1280], replicated, may hold values from -0.3125 to 0.3125
- conv_bias: float32 [1280], replicated, may hold values from -3 to 3
- proj_weight: bfloat16 [1280, 2048], P('dp'), may hold values from -0.15625 to 0.15625
- proj_bias: float32 [2048], replicated, may hold values from -3 to 3
- cotangent: bfloat16 [8, 16384, 2048], P('dp', 'seq'), may hold values from -0.032958984 to 0.032958984
Outputs:
- merged: bfloat16 [8, 16384, 2048], P('dp', 'seq')
- grad_weight: float32 [128, 3, 1280], P('seq', None, 'dp')
Inputs may be any that keep to these rules, and one draw needn't show every extreme that they name: Within a recording the 8192 entries are distinct. Block b of the sequence is positions b * 256 to b * 256 + 255; the 128 tokens of one window put at most 4 entries into any one block, and in each recording one block receives exactly 4 from every window.
All inputs are finite; a program needn't handle non-finite values.
Results may differ from a plain program's by a relative error of at most 0.012.
Values may be sent and summed in bfloat16 or wider, within the bound.
A program may use at most 64 MiB of HBM per device.

v0:
```python
import jax
import jax.numpy as jnp
from jax import lax
from jax.sharding import PartitionSpec as P

SQRT_HALF = 0.7071067811865476
INV_SQRT_TWO_PI = 0.3989422804014327


def body(mel_frames, positions, conv_weight, conv_bias, proj_weight, proj_bias, cotangent):
    frames = mel_frames[0]
    spots = positions[0]
    grads_in = cotangent[0]
    n_own = lax.axis_size("seq")
    n_dp = lax.axis_size("dp")
    frame_count, mels = frames.shape
    tok = frame_count // 2
    rows_own, feats = grads_in.shape
    cap = rows_own // n_own
    taps = conv_weight.shape[1]
    ch = conv_weight.shape[2]
    f32, bf16 = (jnp.float32, jnp.bfloat16)
    full_weight = lax.all_gather(proj_weight, "dp", axis=0, tiled=True)
    padded = jnp.pad(frames, ((1, 1), (0, 0)))
    pairs = padded.reshape(tok + 1, 2 * mels)
    windows = jnp.concatenate([pairs[:-1], pairs[1:]], axis=1)
    owner = spots // rows_own
    row = (spots % rows_own).astype(bf16)
    extra = jnp.concatenate([row[:, None] + 1, jnp.zeros((tok, mels - 1), bf16)], axis=1)
    payload = jnp.concatenate([windows, extra], axis=1)
    earlier = jnp.arange(tok)[None, :] < jnp.arange(tok)[:, None]
    rank = jnp.sum((owner[:, None] == owner[None, :]) & earlier, axis=1)
    slot = owner * cap + rank
    place = (jnp.arange(n_own * cap)[:, None] == slot[None, :]).astype(bf16)
    outgoing = jnp.dot(place, payload, preferred_element_type=f32).astype(bf16)
    arrived = lax.all_to_all(
        outgoing.reshape(n_own, cap, -1), "seq", split_axis=0, concat_axis=0, tiled=True
    ).reshape(n_own * cap, -1)
    arrived_row = arrived[:, 4 * mels].astype(jnp.int32) - 1
    pick = jnp.arange(rows_own)[:, None] == arrived_row[None, :]
    used = jnp.any(pick, axis=1)
    x = jnp.dot(pick.astype(bf16), arrived[:, : 4 * mels], preferred_element_type=f32).astype(bf16)
    kernel = jnp.transpose(conv_weight, (1, 0, 2)).reshape(taps * mels, ch)
    x0, x1 = (x[:, : taps * mels], x[:, mels:])
    pre0 = jnp.dot(x0, kernel, preferred_element_type=f32) + conv_bias
    pre1 = jnp.dot(x1, kernel, preferred_element_type=f32) + conv_bias
    phi0 = 0.5 * (1.0 + lax.erf(pre0 * SQRT_HALF))
    phi1 = 0.5 * (1.0 + lax.erf(pre1 * SQRT_HALF))
    pooled = (0.5 * (pre0 * phi0 + pre1 * phi1)).astype(bf16)
    slope0 = phi0 + pre0 * INV_SQRT_TWO_PI * jnp.exp(-0.5 * pre0 * pre0)
    slope1 = phi1 + pre1 * INV_SQRT_TWO_PI * jnp.exp(-0.5 * pre1 * pre1)
    contract_last = (((1,), (1,)), ((), ()))
    grad_pooled = (
        lax.dot_general(grads_in, full_weight, contract_last, preferred_element_type=f32)
        .astype(bf16)
        .astype(f32)
    )
    g0 = (0.5 * grad_pooled * slope0).astype(bf16)
    g1 = (0.5 * grad_pooled * slope1).astype(bf16)
    contract_first = (((0,), (0,)), ((), ()))
    part = lax.dot_general(x0, g0, contract_first, preferred_element_type=f32) + lax.dot_general(
        x1, g1, contract_first, preferred_element_type=f32
    )
    part = part.astype(bf16).reshape(taps, n_own, mels // n_own, ch)
    part = jnp.transpose(part, (1, 2, 0, 3)).reshape(n_own, -1, ch)
    part = lax.all_to_all(part, "seq", split_axis=0, concat_axis=0, tiled=True)
    part = jnp.sum(part.astype(f32), axis=0).astype(bf16)
    part = jnp.transpose(part.reshape(-1, n_dp, ch // n_dp), (1, 0, 2))
    part = lax.all_to_all(part, "dp", split_axis=0, concat_axis=0, tiled=True)
    grad_weight = jnp.sum(part.astype(f32), axis=0).reshape(mels // n_own, taps, ch // n_dp)
    projected = jnp.dot(pooled, full_weight, preferred_element_type=f32) + proj_bias
    merged = jnp.where(used[:, None], projected, 0.0).astype(bf16)
    return (merged[None], grad_weight)


def solution(mesh):
    in_specs = (
        P("dp", "seq", None),
        P("dp", "seq"),
        P(),
        P(),
        P("dp", None),
        P(),
        P("dp", "seq", None),
    )
    out_specs = (P("dp", "seq", None), P("seq", None, "dp"))
    return jax.shard_map(body, mesh=mesh, in_specs=in_specs, out_specs=out_specs, check_vma=False)
```

profile of v0, /device:TPU:2, one launch (start us, length us, event | category | flops | bytes accessed | tf_op | source)
XLA Modules:
  0.0 159.1 jit_solution(6590703125307992225)
XLA Ops:
  7.2 0.7 all-gather.2.cloned.1.call-update
  7.9 0.7 fusion.42
  8.7 1.0 pad_slice_fusion.1
  9.8 0.7 fusion.55
  10.5 0.7 and_select_fusion.1
  11.3 0.7 fusion.44
  12.0 0.2 convolution_convert_fusion.1
  12.4 27.1 %all_to_all.15 = bf16[64,4,640]{2,1,0:T(4,128)(2,1)S(1)} all-to-all(bf16[64,4,640]{2,1,0:T(4,128)(2,1)S(1)} %reshape.128), channel_id=1, replica_groups=mesh['dp'=8,'seq'=64] {'seq'}, dimensions={0} | all-to-all | bytes 655360 | tf_op jit(solution)/shard_map/all_to_all | solution.py:36
  39.9 1.8 %convolution_add_fusion.1 = f32[256,1280]{1,0:T(8,128)S(1)} fusion(bf16[384,1280]{1,0:T(8,128)(2,1)} %bitcast.35, f32[1280]{0:T(1024)S(1)} %copy-done.4, bf16[256,512]{1,0:T(8,128)(2,1)S(1)} %convolution_convert_fusion.2), kind=kOutput, calls=%fused_computation.1 | convolution fusion | flops 251985920 | bytes 2498560 | tf_op jit(solution)/shard_map/dot_general | solution.py:46
  41.7 1.6 convolution_add_fusion.2
  43.3 38.4 %all-gather.2.cloned.1.call-done = bf16[1280,2048]{1,0:T(8,128)(2,1)} async-done(((bf16[160,2048]{1,0:T(8,128)(2,1)}), bf16[1280,2048]{1,0:T(8,128)(2,1)}) %all-gather.2.cloned.1.call-update) | async-done | bytes 5242896 | tf_op jit(solution)/shard_map/all_gather | solution.py:23
  81.7 4.2 %fusion.4 = f32[256,1280]{1,0:T(8,128)S(1)} fusion(bf16[1280,2048]{1,0:T(8,128)(2,1)} %all-gather.2.cloned.1.call-done, bf16[1,256,2048]{2,1,0:T(8,128)(2,1)S(1)} %copy-done), kind=kOutput, calls=%fused_computation.9 | convolution fusion | flops 1343160320 | bytes 7602176 | tf_op jit(solution)/shard_map/dot_general | solution.py:54
  85.9 0.8 fusion.18
  86.7 1.8 %fusion = bf16[384,1280]{1,0:T(8,128)(2,1)} fusion(f32[384,1280]{1,0:T(8,128)S(1)} %fusion.18, f32[256,1280]{1,0:T(8,128)S(1)} %fusion.4, f32[256,1280]{1,0:T(8,128)S(1)} %convolution_add_fusion.1, bf16[256,512]{1,0:T(8,128)(2,1)S(1)} %convolution_convert_fusion.2), kind=kOutput, calls=%fused_computation.3 | convolution fusion | flops 255918080 | bytes 5767168 | tf_op jit(solution)/shard_map/dot_general | solution.py:61
  88.6 2.4 %reshape.131 = bf16[3,64,2,1280]{3,2,1,0:T(2,128)(2,1)S(1)} reshape(bf16[384,1280]{1,0:T(8,128)(2,1)} %fusion) | data formatting | bytes 1966080 | tf_op jit(solution)/shard_map/reshape | solution.py:64
  91.1 1.7 %copy.28 = bf16[64,6,1280]{2,1,0:T(8,128)(2,1)} copy(bf16[64,6,1280]{2,0,1:T(8,128)(2,1)S(1)} %bitcast.37) | data formatting | bytes 1966080 | tf_op jit(solution)/shard_map/reshape | solution.py:65
  92.8 10.9 %all-to-all-start.1 = ((bf16[64,6,1280]{2,1,0:T(8,128)(2,1)}), bf16[64,6,1280]{2,1,0:T(8,128)(2,1)S(1)}, u32[]{:S(2)}, u32[]{:S(2)}) async-start(bf16[64,6,1280]{2,1,0:T(8,128)(2,1)} %copy.28), calls=%async_computation.1 | async-start | bytes 2621440 | tf_op jit(solution)/shard_map/all_to_all | solution.py:66
  103.9 34.3 %all-to-all-done.1 = bf16[64,6,1280]{2,1,0:T(8,128)(2,1)S(1)} async-done(((bf16[64,6,1280]{2,1,0:T(8,128)(2,1)}), bf16[64,6,1280]{2,1,0:T(8,128)(2,1)S(1)}, u32[]{:S(2)}, u32[]{:S(2)}) %all-to-all-start.1) | async-done | bytes 983072 | tf_op jit(solution)/shard_map/all_to_all | solution.py:66
  138.1 0.3 reduce_sum.34
  138.5 0.7 reshape.136
  139.2 4.5 %all-to-all-start.2 = ((bf16[8,2,480]{2,1,0:T(2,128)(2,1)}), bf16[8,2,480]{2,1,0:T(2,128)(2,1)S(1)}, u32[]{:S(2)}, u32[]{:S(2)}) async-start(bf16[8,2,480]{2,1,0:T(2,128)(2,1)} %reshape.136), calls=%async_computation.2 | async-start | bytes 32768 | tf_op jit(solution)/shard_map/all_to_all | solution.py:69
  143.7 6.1 %fusion.5 = bf16[1,256,2048]{2,1,0:T(8,128)(2,1)} fusion(bf16[1280,2048]{1,0:T(8,128)(2,1)} %all-gather.2.cloned.1.call-done, f32[2048]{0:T(1024)S(1)} %copy-done.5, pred[256]{0:T(512)(128)(4,1)S(1)} %fusion.26, f32[256,1280]{1,0:T(8,128)} %copy-done.1, f32[256,1280]{1,0:T(8,128)} %convolution_add_fusion.2), kind=kOutput, calls=%fused_computation.10 | convolution fusion | flops 1347354624 | bytes 8921344 | tf_op jit(solution)/shard_map/dot_general | solution.py:71
  149.8 1.7 %all-to-all-done.2 = bf16[8,2,480]{2,1,0:T(2,128)(2,1)S(1)} async-done(((bf16[8,2,480]{2,1,0:T(2,128)(2,1)}), bf16[8,2,480]{2,1,0:T(2,128)(2,1)S(1)}, u32[]{:S(2)}, u32[]{:S(2)}) %all-to-all-start.2) | async-done | bytes 15392 | tf_op jit(solution)/shard_map/all_to_all | solution.py:69
  151.6 0.6 copy.30
  (30 shorter events, 1.5 us)
Async XLA Ops:
  7.2 74.6 %copy-start = (bf16[1,256,2048]{2,1,0:T(8,128)(2,1)S(1)}, bf16[1,256,2048]{2,1,0:T(8,128)(2,1)}, u32[]{:S(2)}) copy-start(bf16[1,256,2048]{2,1,0:T(8,128)(2,1)} %param.13) | copy-start | bytes 3145732
  7.2 74.5 %all-gather.2.cloned.1.call-start = ((), (), s32[]{:S(2)}) async-start(), calls=%async_computation.3 | async-start | bytes 5898240 | tf_op jit(solution)/shard_map/all_gather | solution.py:23
  12.3 27.6 %copy-start.4 = (f32[1280]{0:T(1024)S(1)}, f32[1280]{0:T(1024)}, u32[]{:S(2)}) copy-start(f32[1280]{0:T(1024)} %param.10) | copy-start | bytes 15364
  39.9 1.8 %copy-start.3 = (bf16[128,3,1280]{2,0,1:T(8,128)(2,1)S(1)}, bf16[128,3,1280]{2,0,1:T(8,128)(2,1)}, u32[]{:S(2)}) copy-start(bf16[128,3,1280]{2,0,1:T(8,128)(2,1)} %param.9) | copy-start | bytes 2949124
  41.7 45.0 %copy-start.1 = (f32[256,1280]{1,0:T(8,128)}, f32[256,1280]{1,0:T(8,128)S(1)}, u32[]{:S(2)}) copy-start(f32[256,1280]{1,0:T(8,128)S(1)} %convolution_add_fusion.1) | copy-start | bytes 3932164
  81.7 4.2 %copy-start.2 = (f32[256,1280]{1,0:T(8,128)S(1)}, f32[256,1280]{1,0:T(8,128)}, u32[]{:S(2)}) copy-start(f32[256,1280]{1,0:T(8,128)} %convolution_add_fusion.2) | copy-start | bytes 3932164
  92.8 45.3 %all-to-all-start.1 = ((bf16[64,6,1280]{2,1,0:T(8,128)(2,1)}), bf16[64,6,1280]{2,1,0:T(8,128)(2,1)S(1)}, u32[]{:S(2)}, u32[]{:S(2)}) async-start(bf16[64,6,1280]{2,1,0:T(8,128)(2,1)} %copy.28), calls=%async_computation.1 | async-start | bytes 2621440 | tf_op jit(solution)/shard_map/all_to_all | solution.py:66
  103.7 40.0 %copy-start.5 = (f32[2048]{0:T(1024)S(1)}, f32[2048]{0:T(1024)}, u32[]{:S(2)}) copy-start(f32[2048]{0:T(1024)} %param.12) | copy-start | bytes 24580
  139.2 12.2 %all-to-all-start.2 = ((bf16[8,2,480]{2,1,0:T(2,128)(2,1)}), bf16[8,2,480]{2,1,0:T(2,128)(2,1)S(1)}, u32[]{:S(2)}, u32[]{:S(2)}) async-start(bf16[8,2,480]{2,1,0:T(2,128)(2,1)} %reshape.136), calls=%async_computation.2 | async-start | bytes 32768 | tf_op jit(solution)/shard_map/all_to_all | solution.py:69
Sparse Core Ops, SparseCore 0:
  10.1 71.5 all-gather.1
where the time goes:
time: 160 us; the launch traced here: 159 us
  waiting for transfers between devices  75.1 us (47%)
  blocking collectives  27.1 us (17%)
  matrix products  16.7 us (10%)
  starting transfers between devices  15.4 us (10%)
  between operations  14.2 us (9%)
  local copies, waits for them, and re-layouts  7.17 us (4%)
  other arithmetic  3.37 us (2%)
    all_gather x1, waiting for transfers between devices, body(): full_weight = lax.all_gather(proj_weight, 'dp', axis=0, tiled=True)  38.4 us
    all_to_all x1, waiting for transfers between devices, body(): part = lax.all_to_all(part, 'seq', split_axis=0, concat_axis=0, tiled=True)  34.3 us
    all_to_all x1, blocking collectives, body(): lax.all_to_all(outgoing.reshape(n_own, cap, -1), 'seq', split_axis=0, con...  27.1 us
    all_to_all x1, starting transfers between devices, body(): part = lax.all_to_all(part, 'seq', split_axis=0, concat_axis=0, tiled=True)  10.9 us
    dot_general x1, matrix products, body(): jnp.dot(pooled, full_weight, preferred_element_type=f32) + proj_bias  6.07 us
    all_to_all x1, starting transfers between devices, body(): part = lax.all_to_all(part, 'dp', split_axis=0, concat_axis=0, tiled=True)  4.46 us
    dot_general x1, matrix products, body(): lax.dot_general(grads_in, full_weight, contract_last, preferred_element_t...  4.15 us
  transfers between devices with their start and end apart: 3, of which 3 were waited for; matrix products, arithmetic and copies ran while one was open for 9% of the time, Pallas kernels for 0%

commit v1 on v0

--- a/solution.py
+++ b/solution.py
@@ -20,7 +20,9 @@
     taps = conv_weight.shape[1]
     ch = conv_weight.shape[2]
     f32, bf16 = (jnp.float32, jnp.bfloat16)
-    full_weight = lax.all_gather(proj_weight, "dp", axis=0, tiled=True)
+    full_weight = jnp.concatenate(
+        lax.all_to_all(jnp.stack([proj_weight] * lax.axis_size("dp")), "dp", 0, 0), axis=0
+    )
     padded = jnp.pad(frames, ((1, 1), (0, 0)))
     pairs = padded.reshape(tok + 1, 2 * mels)
     windows = jnp.concatenate([pairs[:-1], pairs[1:]], axis=1)

time: 160 us -> 226 us (1.41)
  waiting for transfers between devices: 75.1 us -> 151 us
  between operations: 14.2 us -> 0.84 us
  local copies, waits for them, and re-layouts: 7.17 us -> 10.1 us
    all_to_all x0 -> x1, waiting for transfers between devices: none -> 115 us  [body(): lax.all_to_all(jnp.stack([proj_weight] * lax.axis_size('dp')), 'dp', 0, 0)]
    all_gather x1 -> x0, waiting for transfers between devices: 38.4 us -> none  [body(): full_weight = lax.all_gather(proj_weight, 'dp', axis=0, tiled=True)]
    all_to_all x0 -> x1, starting transfers between devices: none -> 7.23 us  [body(): lax.all_to_all(jnp.stack([proj_weight] * lax.axis_size('dp')), 'dp', 0, 0)]
    all_to_all x1, starting transfers between devices: 10.9 us -> 5.51 us  [body(): part = lax.all_to_all(part, 'seq', split_axis=0, concat_axis=0, tiled=True)]
    another operation x0 -> x1, local copies, waits for them, and re-layouts: none -> 3.01 us  [body(): jnp.stack([proj_weight] * lax.axis_size('dp'))]
  transfers between devices with their start and end apart: 3 -> 3, of which waited for: 3 -> 3; matrix products, arithmetic and copies ran while one was open for 9% -> 4% of each run, Pallas kernels for 0% -> 0%
where the time goes in v1:
time: 226 us
  waiting for transfers between devices  151 us (67%)
  blocking collectives  27.1 us (12%)
  matrix products  16.7 us (7%)
  starting transfers between devices  16.1 us (7%)
  local copies, waits for them, and re-layouts  10.1 us (4%)
  other arithmetic  3.49 us (2%)
    all_to_all x1, waiting for transfers between devices, body(): lax.all_to_all(jnp.stack([proj_weight] * lax.axis_size('dp')), 'dp', 0, 0)  115 us
    all_to_all x1, waiting for transfers between devices, body(): part = lax.all_to_all(part, 'seq', split_axis=0, concat_axis=0, tiled=True)  34.3 us
    all_to_all x1, blocking collectives, body(): lax.all_to_all(outgoing.reshape(n_own, cap, -1), 'seq', split_axis=0, con...  27.1 us
    all_to_all x1, starting transfers between devices, body(): lax.all_to_all(jnp.stack([proj_weight] * lax.axis_size('dp')), 'dp', 0, 0)  7.23 us
    dot_general x1, matrix products, body(): jnp.dot(pooled, full_weight, preferred_element_type=f32) + proj_bias  6.07 us
    all_to_all x1, starting transfers between devices, body(): part = lax.all_to_all(part, 'seq', split_axis=0, concat_axis=0, tiled=True)  5.51 us
  transfers between devices with their start and end apart: 3, of which 3 were waited for; matrix products, arithmetic and copies ran while one was open for 4% of the time, Pallas kernels for 0%

profile of v1, /device:TPU:2, one launch (start us, length us, event | category | flops | bytes accessed | tf_op | source)
XLA Modules:
  0.0 225.7 jit_solution(6448487089758118575)
XLA Ops:
  0.7 0.8 fusion.42
  1.4 0.7 fusion.55
  2.1 0.7 and_select_fusion.1
  2.9 1.0 pad_slice_fusion.1
  4.1 0.7 fusion.44
  5.2 27.1 %all_to_all.20 = bf16[64,4,640]{2,1,0:T(4,128)(2,1)S(1)} all-to-all(bf16[64,4,640]{2,1,0:T(4,128)(2,1)S(1)} %reshape.133), channel_id=1, replica_groups=mesh['dp'=8,'seq'=64] {'seq'}, dimensions={0} | all-to-all | bytes 655360 | tf_op jit(solution)/shard_map/all_to_all | solution.py:38
  32.3 3.0 %stack.2 = bf16[8,160,2048]{2,1,0:T(8,128)(2,1)} broadcast(bf16[160,2048]{1,0:T(8,128)(2,1)S(1)} %copy-done.4), dimensions={1,2} | broadcast | bytes 5898240 | tf_op jit(solution)/shard_map/stack | solution.py:24
  35.3 7.2 %all-to-all-start.1 = ((bf16[8,160,2048]{2,1,0:T(8,128)(2,1)}), bf16[8,160,2048]{2,1,0:T(8,128)(2,1)}, u32[]{:S(2)}, u32[]{:S(2)}) async-start(bf16[8,160,2048]{2,1,0:T(8,128)(2,1)} %stack.2), calls=%async_computation.1 | async-start | bytes 10485760 | tf_op jit(solution)/shard_map/all_to_all | solution.py:24
  43.0 1.8 convolution_add_fusion.1
  44.8 1.6 convolution_add_fusion.2
  46.4 115.4 %all-to-all-done.1 = bf16[8,160,2048]{2,1,0:T(8,128)(2,1)} async-done(((bf16[8,160,2048]{2,1,0:T(8,128)(2,1)}), bf16[8,160,2048]{2,1,0:T(8,128)(2,1)}, u32[]{:S(2)}, u32[]{:S(2)}) %all-to-all-start.1) | async-done | bytes 5242912 | tf_op jit(solution)/shard_map/all_to_all | solution.py:24
  161.9 4.1 %fusion.4 = f32[256,1280]{1,0:T(8,128)S(1)} fusion(bf16[1280,2048]{1,0:T(8,128)(2,1)} %bitcast.9, bf16[1,256,2048]{2,1,0:T(8,128)(2,1)S(1)} %copy-done), kind=kOutput, calls=%fused_computation.9 | convolution fusion | flops 1343160320 | bytes 7602176 | tf_op jit(solution)/shard_map/dot_general | solution.py:56
  166.0 0.8 fusion.18
  166.9 1.8 fusion
  168.7 2.4 %reshape.137 = bf16[3,64,2,1280]{3,2,1,0:T(2,128)(2,1)S(1)} reshape(bf16[384,1280]{1,0:T(8,128)(2,1)} %fusion) | data formatting | bytes 1966080 | tf_op jit(solution)/shard_map/reshape | solution.py:66
  171.2 1.7 copy.28
  172.9 5.5 %all-to-all-start.2 = ((bf16[64,6,1280]{2,1,0:T(8,128)(2,1)}), bf16[64,6,1280]{2,1,0:T(8,128)(2,1)S(1)}, u32[]{:S(2)}, u32[]{:S(2)}) async-start(bf16[64,6,1280]{2,1,0:T(8,128)(2,1)} %copy.28), calls=%async_computation.2 | async-start | bytes 2621440 | tf_op jit(solution)/shard_map/all_to_all | solution.py:68
  178.5 34.3 %all-to-all-done.2 = bf16[64,6,1280]{2,1,0:T(8,128)(2,1)S(1)} async-done(((bf16[64,6,1280]{2,1,0:T(8,128)(2,1)}), bf16[64,6,1280]{2,1,0:T(8,128)(2,1)S(1)}, u32[]{:S(2)}, u32[]{:S(2)}) %all-to-all-start.2) | async-done | bytes 983072 | tf_op jit(solution)/shard_map/all_to_all | solution.py:68
  212.8 0.3 reduce_sum.34
  213.2 0.7 reshape.142
  213.9 3.3 %all-to-all-start.3 = ((bf16[8,2,480]{2,1,0:T(2,128)(2,1)}), bf16[8,2,480]{2,1,0:T(2,128)(2,1)S(1)}, u32[]{:S(2)}, u32[]{:S(2)}) async-start(bf16[8,2,480]{2,1,0:T(2,128)(2,1)} %reshape.142), calls=%async_computation.3 | async-start | bytes 32768 | tf_op jit(solution)/shard_map/all_to_all | solution.py:71
  217.2 6.1 %fusion.5 = bf16[1,256,2048]{2,1,0:T(8,128)(2,1)} fusion(bf16[1280,2048]{1,0:T(8,128)(2,1)} %bitcast.9, f32[2048]{0:T(1024)S(1)} %copy-done.6, pred[256]{0:T(512)(128)(4,1)S(1)} %fusion.26, f32[256,1280]{1,0:T(8,128)} %copy-done.1, f32[256,1280]{1,0:T(8,128)} %convolution_add_fusion.2), kind=kOutput, calls=%fused_computation.10 | convolution fusion | flops 1347354624 | bytes 8921344 | tf_op jit(solution)/shard_map/dot_general | solution.py:73
  223.3 1.6 all-to-all-done.3
  225.1 0.6 copy.30
  (32 shorter events, 1.7 us)
Async XLA Ops:
  0.6 161.2 %copy-start = (bf16[1,256,2048]{2,1,0:T(8,128)(2,1)S(1)}, bf16[1,256,2048]{2,1,0:T(8,128)(2,1)}, u32[]{:S(2)}) copy-start(bf16[1,256,2048]{2,1,0:T(8,128)(2,1)} %param.13) | copy-start | bytes 3145732
  0.6 31.7 %copy-start.4 = (bf16[160,2048]{1,0:T(8,128)(2,1)S(1)}, bf16[160,2048]{1,0:T(8,128)(2,1)}, u32[]{:S(2)}) copy-start(bf16[160,2048]{1,0:T(8,128)(2,1)} %param.11) | copy-start | bytes 1966084
  35.3 7.7 %copy-start.5 = (f32[1280]{0:T(1024)S(1)}, f32[1280]{0:T(1024)}, u32[]{:S(2)}) copy-start(f32[1280]{0:T(1024)} %param.10) | copy-start | bytes 15364
  35.3 126.5 %all-to-all-start.1 = ((bf16[8,160,2048]{2,1,0:T(8,128)(2,1)}), bf16[8,160,2048]{2,1,0:T(8,128)(2,1)}, u32[]{:S(2)}, u32[]{:S(2)}) async-start(bf16[8,160,2048]{2,1,0:T(8,128)(2,1)} %stack.2), calls=%async_computation.1 | async-start | bytes 10485760 | tf_op jit(solution)/shard_map/all_to_all | solution.py:24
  43.0 1.8 copy-start.3
  44.8 122.0 %copy-start.1 = (f32[256,1280]{1,0:T(8,128)}, f32[256,1280]{1,0:T(8,128)S(1)}, u32[]{:S(2)}) copy-start(f32[256,1280]{1,0:T(8,128)S(1)} %convolution_add_fusion.1) | copy-start | bytes 3932164
  161.9 4.2 %copy-start.2 = (f32[256,1280]{1,0:T(8,128)S(1)}, f32[256,1280]{1,0:T(8,128)}, u32[]{:S(2)}) copy-start(f32[256,1280]{1,0:T(8,128)} %convolution_add_fusion.2) | copy-start | bytes 3932164
  172.9 39.9 %all-to-all-start.2 = ((bf16[64,6,1280]{2,1,0:T(8,128)(2,1)}), bf16[64,6,1280]{2,1,0:T(8,128)(2,1)S(1)}, u32[]{:S(2)}, u32[]{:S(2)}) async-start(bf16[64,6,1280]{2,1,0:T(8,128)(2,1)} %copy.28), calls=%async_computation.2 | async-start | bytes 2621440 | tf_op jit(solution)/shard_map/all_to_all | solution.py:68
  178.4 38.9 %copy-start.6 = (f32[2048]{0:T(1024)S(1)}, f32[2048]{0:T(1024)}, u32[]{:S(2)}) copy-start(f32[2048]{0:T(1024)} %param.12) | copy-start | bytes 24580
  213.9 11.0 %all-to-all-start.3 = ((bf16[8,2,480]{2,1,0:T(2,128)(2,1)}), bf16[8,2,480]{2,1,0:T(2,128)(2,1)S(1)}, u32[]{:S(2)}, u32[]{:S(2)}) async-start(bf16[8,2,480]{2,1,0:T(2,128)(2,1)} %reshape.142), calls=%async_computation.3 | async-start | bytes 32768 | tf_op jit(solution)/shard_map/all_to_all | solution.py:71
